TPU v7x, 256 devices: a whole 4x4x8 slice. The times are simulated.
256 devices in a mesh: cols: 32 (over y, z), mem: 8 (over x, core).
Axes of the slice: x: 4, y: 4, z: 8, core: 2. Of those that a mesh axis runs over, the one named last changes fastest.
Arguments:
- state: float32 [80, 1048576], P('mem', 'cols'), may hold values from -6 to 6
- obs_value: float32 [4, 1024], P(None, 'cols'), may hold values from -6 to 6
- obs_var: float32 [4, 1024], P(None, 'cols'), may hold values from 0.2 to 2
- owner: int32 [4, 1024, 1], P(None, 'cols'), may hold values from 0 to 31; in each aligned block of 32 rows (0 to 31, 32 to 63, ..., all dimensions but the last counted through in order) at most 2 rows name the same one
- tile_of: int32 [4, 1024], P(None, 'cols'), may hold values from 0 to 63
- offsets: int32 [4, 1024, 4], P(None, 'cols'), may hold values from 0 to 511
- accept: int32 [4, 1024], P(None, 'cols'), may hold values 0 or 1
- loc_mask: int32 [2048, 4, 8], P(('cols', 'mem')), may hold values 0 or 1
Outputs:
- posterior: float32 [80, 1048576], P(None, ('cols', 'mem'))
Inputs may be any that keep to these rules, and one draw needn't show every extreme that they name: Within the 32 observations of one batch held by one index of cols, no owner is named more than 2 times, and that many is reached.
All inputs are finite; a program needn't handle non-finite values. No bound on the sum of `accept` or of `loc_mask` on one device may be relied on, other than what follows from the above.
Results may differ from a plain program's by a relative error of at most 0.0002.
Values sent between devices are 32-bit elements; how exact they have to be, the bound alone decides.
A program may use at most 64 MiB of HBM per device.

v0:
```python
import jax
import jax.numpy as jnp
from jax import lax
from jax.sharding import PartitionSpec as P

epsilon = 1e-05
EXACT = lax.Precision.HIGHEST


def innovations(prior_obs, observed, obs_noise, accepted):
    members = prior_obs.shape[0]
    mean_prior = jnp.mean(prior_obs, axis=0)
    spread = prior_obs - mean_prior
    spread_var = jnp.sum(spread * spread, axis=0) / (members - 1) + epsilon
    denominator = spread_var + obs_noise
    mean_shift = spread_var / denominator * (observed - mean_prior)
    factor = jnp.sqrt(obs_noise / denominator) - 1.0
    increment = accepted * (mean_shift + factor * spread)
    scaled = spread / ((members - 1) * spread_var)
    return (increment, scaled)


def local(state, obs_value, obs_var, owner, tile_of, offsets, accept, loc_mask):
    col_devices = lax.axis_size("cols")
    mem_devices = lax.axis_size("mem")
    source = lax.axis_index("cols")
    mem_index = lax.axis_index("mem")
    batch_total, per_src = obs_value.shape
    pick_count = offsets.shape[2]
    members = state.shape[0] * mem_devices
    cell_count = state.shape[1] // mem_devices
    tiles_here = loc_mask.shape[0]
    tile_len = cell_count // tiles_here
    block_count = loc_mask.shape[2]
    batch_obs = per_src * col_devices
    block_len = batch_obs // block_count
    capacity = max(2, 2 * per_src // col_devices)
    slot_count = col_devices * capacity
    destination = owner[:, :, 0]
    ordinal = jnp.arange(per_src, dtype=jnp.int32)
    same_owner = destination[:, :, None] == destination[:, None, :]
    earlier = (ordinal[None, :] < ordinal[:, None])[None]
    slot_rank = jnp.sum((same_owner & earlier).astype(jnp.int32), axis=2)
    batch_rows = jnp.broadcast_to(
        jnp.arange(batch_total, dtype=jnp.int32)[:, None], destination.shape
    )
    position = jnp.broadcast_to(source * per_src + ordinal, destination.shape)
    fields = jnp.concatenate(
        [tile_of[:, :, None], accept[:, :, None], position[:, :, None], offsets], axis=2
    )
    blank_int = (
        jnp.zeros((batch_total, col_devices, capacity, 3 + pick_count), jnp.int32)
        .at[:, :, :, 2]
        .set(-1)
    )
    sent_int = blank_int.at[batch_rows, destination, slot_rank].set(fields)
    blank_val = (
        jnp.zeros((batch_total, col_devices, capacity, 2), jnp.float32).at[:, :, :, 1].set(1.0)
    )
    sent_val = blank_val.at[batch_rows, destination, slot_rank].set(
        jnp.stack([obs_value, obs_var], axis=2)
    )
    arrived_int = lax.all_to_all(sent_int, "cols", split_axis=1, concat_axis=1, tiled=True).reshape(
        batch_total, slot_count, 3 + pick_count
    )
    arrived_val = lax.all_to_all(sent_val, "cols", split_axis=1, concat_axis=1, tiled=True).reshape(
        batch_total, slot_count, 2
    )
    obs_tile = arrived_int[:, :, 0]
    obs_flag = arrived_int[:, :, 1].astype(jnp.float32)
    obs_pos = arrived_int[:, :, 2]
    obs_off = arrived_int[:, :, 3:]
    observed = arrived_val[:, :, 0]
    obs_noise = arrived_val[:, :, 1]
    targets = jnp.where(obs_pos >= 0, obs_pos, batch_obs)
    ensemble = lax.all_to_all(state, "mem", split_axis=1, concat_axis=0, tiled=True)
    for batch_no in range(batch_total):
        local_cell = (
            obs_tile[batch_no][:, None] * tile_len + obs_off[batch_no] - mem_index * cell_count
        )
        inside = (local_cell >= 0) & (local_cell < cell_count) & (obs_pos[batch_no] >= 0)[:, None]
        flat_cells = jnp.clip(local_cell, 0, cell_count - 1).reshape(-1)
        picked = jnp.take(ensemble, flat_cells, axis=1).reshape(members, slot_count, pick_count)
        prior_obs = lax.psum(
            jnp.sum(jnp.where(inside[None], picked, 0.0), axis=2) / pick_count, "mem"
        )
        increment, scaled = innovations(
            prior_obs, observed[batch_no], obs_noise[batch_no], obs_flag[batch_no]
        )
        blank_panel = jnp.zeros((members, batch_obs), jnp.float32)
        placed_inc = blank_panel.at[:, targets[batch_no]].add(increment, mode="drop")
        placed_scl = blank_panel.at[:, targets[batch_no]].add(scaled, mode="drop")
        inc_all, scl_all = lax.psum((placed_inc, placed_scl), "cols")
        mask_now = loc_mask[:, batch_no, :].astype(jnp.float32)
        mean_state = jnp.mean(ensemble, axis=0)
        deviation = (ensemble - mean_state).reshape(members, tiles_here, tile_len)
        per_block = jnp.einsum(
            "nbk,mbk->bnm",
            scl_all.reshape(members, block_count, block_len),
            inc_all.reshape(members, block_count, block_len),
            precision=EXACT,
        )
        mixing = jnp.einsum("tb,bnm->tnm", mask_now, per_block, precision=EXACT)
        change = jnp.einsum("tnm,nti->mti", mixing, deviation, precision=EXACT).reshape(
            members, cell_count
        )
        ensemble = ensemble + change
    return ensemble


def solution(mesh):
    return jax.shard_map(
        local,
        mesh=mesh,
        in_specs=(
            P("mem", "cols"),
            P(None, "cols"),
            P(None, "cols"),
            P(None, "cols", None),
            P(None, "cols"),
            P(None, "cols", None),
            P(None, "cols"),
            P(("cols", "mem"), None, None),
        ),
        out_specs=P(None, ("cols", "mem")),
        check_vma=False,
    )
```

profile of v0, /device:TPU:2, one launch (start us, length us, event | category | flops | bytes accessed | tf_op | source)
XLA Modules:
  0.0 843.9 jit_solution(13650649832202001526)
XLA Ops:
  10.0 7.9 scatter_fusion.1
  19.1 11.5 %all-to-all-start.2 = ((f32[4,32,2,2]{0,3,2,1:T(2,128)}), f32[4,32,2,2]{0,3,2,1:T(2,128)S(1)}, u32[]{:S(2)}, u32[]{:S(2)}) async-start(f32[4,32,2,2]{0,3,2,1:T(2,128)} %copy.270), calls=%async_computation.2 | async-start | bytes 131072 | tf_op jit(solution)/shard_map/all_to_all | solution.py:66
  31.4 7.9 scatter_fusion
  40.0 1.2 copy.348
  41.3 2.2 copy.253
  43.5 9.8 %all-to-all-start.1 = ((s32[4,32,2,7]{3,2,0,1:T(2,128)}), s32[4,32,2,7]{3,2,0,1:T(2,128)S(1)}, u32[]{:S(2)}, u32[]{:S(2)}) async-start(s32[4,32,2,7]{3,2,0,1:T(2,128)} %copy.261), calls=%async_computation.1 | async-start | bytes 262144 | tf_op jit(solution)/shard_map/all_to_all | solution.py:63
  54.2 9.5 %all-to-all-done.1 = s32[4,32,2,7]{3,2,0,1:T(2,128)S(1)} async-done(((s32[4,32,2,7]{3,2,0,1:T(2,128)}), s32[4,32,2,7]{3,2,0,1:T(2,128)S(1)}, u32[]{:S(2)}, u32[]{:S(2)}) %all-to-all-start.1) | async-done | bytes 7200 | tf_op jit(solution)/shard_map/all_to_all | solution.py:63
  63.7 4.8 all-to-all-start
  75.7 18.6 %all-to-all-done = f32[10,8,4096]{2,0,1:T(8,128)S(1)} async-done(((f32[10,8,4096]{2,0,1:T(8,128)}), f32[10,8,4096]{2,0,1:T(8,128)S(1)}, u32[]{:S(2)}, u32[]{:S(2)}) %all-to-all-start) | async-done | bytes 1310752 | tf_op jit(solution)/shard_map/all_to_all | solution.py:76
  94.5 1.8 copy.266
  96.3 2.4 gather_fusion
  99.8 21.7 %psum.84 = f32[80,64]{0,1:T(8,128)S(1)} all-reduce(f32[80,64]{0,1:T(8,128)S(1)} %broadcast_multiply_fusion.3), channel_id=1, replica_groups=mesh['cols'=32,'mem'=8] {'mem'}, use_global_device_ids=true, to_apply=%region_4.6 | all-reduce | flops 5120 | bytes 40960 | tf_op jit(solution)/shard_map/psum | solution.py:84
  122.5 1.2 scatter_custom_fusion.3
  131.7 1.3 broadcast_subtract_fusion
  133.0 139.0 %all-reduce.15.cloned.1.call-done = (f32[80,8,128]{2,0,1:T(8,128)}, f32[80,8,128]{2,0,1:T(8,128)}) async-done(((f32[80,8,128]{2,0,1:T(8,128)}, f32[80,8,128]{2,0,1:T(8,128)}), (f32[80,8,128]{2,0,1:T(8,128)}, f32[80,8,128]{2,0,1:T(8,128)})) %all-reduce.15.cloned.1.call-update) | async-done | bytes 655376 | tf_op jit(solution)/shard_map/psum | solution.py:93
  272.0 1.8 fusion.125
  274.4 2.1 fusion
  276.6 1.2 copy-done.4
  277.8 1.2 add.373
  279.0 2.8 copy.284
  281.8 2.4 gather_fusion.1
  285.3 20.7 %psum.87 = f32[80,64]{0,1:T(8,128)S(1)} all-reduce(f32[80,64]{0,1:T(8,128)S(1)} %broadcast_multiply_fusion.2), channel_id=1, replica_groups=mesh['cols'=32,'mem'=8] {'mem'}, use_global_device_ids=true, to_apply=%region_14.16 | all-reduce | flops 5120 | bytes 40960 | tf_op jit(solution)/shard_map/psum | solution.py:84
  307.0 1.8 scatter_custom_fusion.5
  308.8 2.0 copy.288
  310.7 1.8 scatter_custom_fusion.4
  312.5 2.0 copy.286
  316.7 1.8 copy.278
  318.5 2.7 reshape.653
  321.2 1.9 add_reduce_fusion
  323.1 138.9 %all-reduce.13.cloned.1.call-done = (f32[80,8,128]{2,0,1:T(8,128)}, f32[80,8,128]{2,0,1:T(8,128)}) async-done(((f32[80,8,128]{2,0,1:T(8,128)}, f32[80,8,128]{2,0,1:T(8,128)}), (f32[80,8,128]{2,0,1:T(8,128)}, f32[80,8,128]{2,0,1:T(8,128)})) %all-reduce.13.cloned.1.call-update) | async-done | bytes 655376 | tf_op jit(solution)/shard_map/psum | solution.py:93
  462.1 1.7 fusion.126
  464.3 3.9 fusion.122
  468.3 1.2 copy-done.5
  473.2 20.7 %psum.90 = f32[80,64]{0,1:T(8,128)S(1)} all-reduce(f32[80,64]{0,1:T(8,128)S(1)} %broadcast_multiply_fusion.1), channel_id=1, replica_groups=mesh['cols'=32,'mem'=8] {'mem'}, use_global_device_ids=true, to_apply=%region_23.25 | all-reduce | flops 5120 | bytes 40960 | tf_op jit(solution)/shard_map/psum | solution.py:84
  499.3 147.3 %all-reduce.11.cloned.1.call-done = (f32[80,8,128]{2,0,1:T(8,128)}, f32[80,8,128]{2,0,1:T(8,128)}) async-done(((f32[80,8,128]{2,0,1:T(8,128)}, f32[80,8,128]{2,0,1:T(8,128)}), (f32[80,8,128]{2,0,1:T(8,128)}, f32[80,8,128]{2,0,1:T(8,128)})) %all-reduce.11.cloned.1.call-update) | async-done | bytes 655376 | tf_op jit(solution)/shard_map/psum | solution.py:93
  646.6 1.7 fusion.127
  648.8 1.4 fusion.10
  650.4 1.2 copy-done.7
  651.5 1.2 add.398
  652.8 2.8 copy.308
  655.6 2.3 gather_fusion.3
  658.2 20.7 %psum.93 = f32[80,64]{0,1:T(8,128)S(1)} all-reduce(f32[80,64]{0,1:T(8,128)S(1)} %broadcast_multiply_fusion), channel_id=1, replica_groups=mesh['cols'=32,'mem'=8] {'mem'}, use_global_device_ids=true, to_apply=%region_32.34 | all-reduce | flops 5120 | bytes 40960 | tf_op jit(solution)/shard_map/psum | solution.py:84
  679.2 1.4 scatter_custom_fusion.9
  683.7 147.6 %all-reduce.9.cloned.1.call-done = (f32[80,8,128]{2,0,1:T(8,128)}, f32[80,8,128]{2,0,1:T(8,128)}) async-done(((f32[80,8,128]{2,0,1:T(8,128)}, f32[80,8,128]{2,0,1:T(8,128)}), (f32[80,8,128]{2,0,1:T(8,128)}, f32[80,8,128]{2,0,1:T(8,128)})) %all-reduce.9.cloned.1.call-update) | async-done | bytes 655376 | tf_op jit(solution)/shard_map/psum | solution.py:93
  831.2 1.7 fusion.128
  833.5 1.4 convolution_bitcast_fusion
  835.0 1.2 copy-done.8
  836.2 1.2 add.410
  (200 shorter events, 43.2 us)
Async XLA Ops:
  6.5 24.8 %copy-start.10 = (s32[4,32,2,7]{3,2,1,0:T(2,128)S(1)}, s32[4,32,2,7]{3,2,1,0:T(2,128)}, u32[]{:S(2)}) copy-start(s32[4,32,2,7]{3,2,1,0:T(2,128)} %constant.122.clone.1) | copy-start | bytes 21508
  6.5 24.1 %copy-start.18 = (s32[8,4,8]{2,1,0:T(4,128)S(1)}, s32[8,4,8]{2,1,0:T(4,128)}, u32[]{:S(2)}) copy-start(s32[8,4,8]{2,1,0:T(4,128)} %param.21) | copy-start | bytes 3076
  6.5 24.7 %copy-start.40 = (s32[4,32]{1,0:T(4,128)S(1)}, s32[4,32]{1,0:T(4,128)}, u32[]{:S(2)}) copy-start(s32[4,32]{1,0:T(4,128)} %param.20) | copy-start | bytes 1540
  6.5 24.7 %copy-start.21 = (s32[4,32,4]{1,2,0:T(4,128)S(1)}, s32[4,32,4]{1,2,0:T(4,128)}, u32[]{:S(2)}) copy-start(s32[4,32,4]{1,2,0:T(4,128)} %param.19) | copy-start | bytes 6148
  6.5 24.7 %copy-start.41 = (s32[4,32]{1,0:T(4,128)S(1)}, s32[4,32]{1,0:T(4,128)}, u32[]{:S(2)}) copy-start(s32[4,32]{1,0:T(4,128)} %param.18) | copy-start | bytes 1540
  18.0 22.0 %copy-start.11 = (f32[10,32768]{1,0:T(8,128)S(1)}, f32[10,32768]{1,0:T(8,128)}, u32[]{:S(2)}) copy-start(f32[10,32768]{1,0:T(8,128)} %param.14) | copy-start | bytes 3932164
  19.1 24.4 %all-to-all-start.2 = ((f32[4,32,2,2]{0,3,2,1:T(2,128)}), f32[4,32,2,2]{0,3,2,1:T(2,128)S(1)}, u32[]{:S(2)}, u32[]{:S(2)}) async-start(f32[4,32,2,2]{0,3,2,1:T(2,128)} %copy.270), calls=%async_computation.2 | async-start | bytes 131072 | tf_op jit(solution)/shard_map/all_to_all | solution.py:66
  43.5 20.2 %all-to-all-start.1 = ((s32[4,32,2,7]{3,2,0,1:T(2,128)}), s32[4,32,2,7]{3,2,0,1:T(2,128)S(1)}, u32[]{:S(2)}, u32[]{:S(2)}) async-start(s32[4,32,2,7]{3,2,0,1:T(2,128)} %copy.261), calls=%async_computation.1 | async-start | bytes 262144 | tf_op jit(solution)/shard_map/all_to_all | solution.py:63
  63.7 30.5 %all-to-all-start = ((f32[10,8,4096]{2,0,1:T(8,128)}), f32[10,8,4096]{2,0,1:T(8,128)S(1)}, u32[]{:S(2)}, u32[]{:S(2)}) async-start(f32[10,8,4096]{2,0,1:T(8,128)} %copy.253), calls=%async_computation | async-start | bytes 4194304 | tf_op jit(solution)/shard_map/all_to_all | solution.py:76
  68.6 203.5 %all-reduce.15.cloned.1.call-start = ((), (), s32[]{:S(2)}) async-start(), calls=%async_computation.6 | async-start | bytes 1310720 | tf_op jit(solution)/shard_map/psum | solution.py:93
  70.2 24.1 %copy-start.12 = (s32[1,64,4]{2,1,0:T(8,128)}, s32[1,64,4]{2,1,0:T(8,128)S(1)}, u32[]{:S(2)}) copy-start(s32[1,64,4]{2,1,0:T(8,128)S(1)} %get-tuple-element.71) | copy-start | bytes 3076
  70.2 24.1 %copy-start.14 = (s32[1,64,4]{2,1,0:T(8,128)}, s32[1,64,4]{2,1,0:T(8,128)S(1)}, u32[]{:S(2)}) copy-start(s32[1,64,4]{2,1,0:T(8,128)S(1)} %get-tuple-element.68) | copy-start | bytes 3076
  94.5 1.9 copy-start.3
  123.7 3.3 copy-start.19
  123.7 3.3 copy-start.20
  123.7 3.3 copy-start.22
  123.7 3.3 copy-start.23
  123.7 3.3 copy-start.35
  123.7 3.3 copy-start.36
  123.7 3.9 copy-start.15
  123.7 4.5 copy-start.13
  124.7 5.8 copy-start.38
  124.7 5.9 copy-start.24
  126.8 335.3 %all-reduce.13.cloned.1.call-start = ((), (), s32[]{:S(2)}) async-start(), calls=%async_computation.5 | async-start | bytes 1310720 | tf_op jit(solution)/shard_map/psum | solution.py:93
  131.5 1.5 copy-start.1
  272.0 2.3 copy-start.9
  276.5 1.3 copy-start.4
  281.8 25.1 %copy-start.31 = (f32[64]{0:T(128)S(1)}, f32[64]{0:T(128)}, u32[]{:S(2)}) copy-start(f32[64]{0:T(128)} %get-tuple-element.32) | copy-start | bytes 772
  308.8 6.0 copy-start.25
  308.8 6.0 copy-start.27
  308.8 6.0 copy-start.28
  308.8 6.0 copy-start.29
  308.8 6.6 copy-start.39
  314.5 332.1 %all-reduce.11.cloned.1.call-start = ((), (), s32[]{:S(2)}) async-start(), calls=%async_computation.4 | async-start | bytes 1310720 | tf_op jit(solution)/shard_map/psum | solution.py:93
  323.1 141.2 %copy-start.2 = (f32[80,8,512]{2,1,0:T(8,128)S(1)}, f32[80,8,512]{2,1,0:T(8,128)}, u32[]{:S(2)}) copy-start(f32[80,8,512]{2,1,0:T(8,128)} %copy-done.1) | copy-start | bytes 3932164
  468.2 1.3 copy-start.5
  496.0 3.1 copy-start.37
  496.0 3.2 copy-start.26
  498.1 150.2 %copy-start.17 = (s32[8,1,8]{2,1,0:T(1,128)S(1)}, s32[8,1,8]{2,1,0:T(1,128)}, u32[]{:S(2)}) copy-start(s32[8,1,8]{2,1,0:T(1,128)} %get-tuple-element.75) | copy-start | bytes 772
  499.0 149.8 %copy-start = (f32[80,8,512]{2,0,1:T(8,128)S(1)}, f32[80,8,512]{2,0,1:T(8,128)}, u32[]{:S(2)}) copy-start(f32[80,8,512]{2,0,1:T(8,128)} %get-tuple-element.63) | copy-start | bytes 3932164
  499.1 332.2 %all-reduce.9.cloned.1.call-start = ((), (), s32[]{:S(2)}) async-start(), calls=%async_computation.3 | async-start | bytes 1310720 | tf_op jit(solution)/shard_map/psum | solution.py:93
  650.2 1.3 copy-start.7
  652.8 5.1 copy-start.34
  655.6 23.6 %copy-start.32 = (f32[64]{0:T(128)S(1)}, f32[64]{0:T(128)}, u32[]{:S(2)}) copy-start(f32[64]{0:T(128)} %get-tuple-element.42) | copy-start | bytes 772
  655.6 23.6 %copy-start.33 = (f32[64]{0:T(128)S(1)}, f32[64]{0:T(128)}, u32[]{:S(2)}) copy-start(f32[64]{0:T(128)} %get-tuple-element.43) | copy-start | bytes 772
  655.6 23.7 %copy-start.30 = (f32[64]{0:T(128)S(1)}, f32[64]{0:T(128)}, u32[]{:S(2)}) copy-start(f32[64]{0:T(128)} %get-tuple-element.30) | copy-start | bytes 772
  682.7 150.3 %copy-start.16 = (s32[8,1,8]{2,1,0:T(1,128)S(1)}, s32[8,1,8]{2,1,0:T(1,128)}, u32[]{:S(2)}) copy-start(s32[8,1,8]{2,1,0:T(1,128)} %get-tuple-element.74) | copy-start | bytes 772
  834.9 1.3 copy-start.8
  (1 other events, 1.1 us)
Sparse Core Ops, SparseCore 0:
  126.9 145.1 all-reduce.14
  314.6 147.3 all-reduce.12
  499.2 147.3 all-reduce.10
  683.8 147.4 all-reduce.8
where the time goes:
time: 845 us; the launch traced here: 844 us
  waiting for transfers between devices  601 us (71%)
  blocking collectives  83.8 us (10%)
  local copies, waits for them, and re-layouts  67.1 us (8%)
  other arithmetic  33.7 us (4%)
  starting transfers between devices  26.6 us (3%)
  matrix products  17.7 us (2%)
  between operations  14.1 us (2%)
    psum x4, waiting for transfers between devices, local(): inc_all, scl_all = lax.psum((placed_inc, placed_scl), 'cols')  573 us
    psum x4, blocking collectives, local(): lax.psum(jnp.sum(jnp.where(inside[None], picked, 0.0), axis=2) / pick_cou...  83.8 us
    all_to_all x1, waiting for transfers between devices, local(): lax.all_to_all(state, 'mem', split_axis=1, concat_axis=0, tiled=True)  18.6 us
  transfers between devices with their start and end apart: 7, of which 6 were waited for; matrix products, arithmetic and copies ran while one was open for 4% of the time, Pallas kernels for 0%

commit v1 on v0

--- a/solution.py
+++ b/solution.py
@@ -81,9 +81,9 @@
         inside = (local_cell >= 0) & (local_cell < cell_count) & (obs_pos[batch_no] >= 0)[:, None]
         flat_cells = jnp.clip(local_cell, 0, cell_count - 1).reshape(-1)
         picked = jnp.take(ensemble, flat_cells, axis=1).reshape(members, slot_count, pick_count)
-        prior_obs = lax.psum(
-            jnp.sum(jnp.where(inside[None], picked, 0.0), axis=2) / pick_count, "mem"
-        )
+        x = jnp.sum(jnp.where(inside[None], picked, 0.0), axis=2) / pick_count
+        shards = lax.all_gather(x, "mem", axis=0, tiled=False)
+        prior_obs = shards.sum(axis=0)
         increment, scaled = innovations(
             prior_obs, observed[batch_no], obs_noise[batch_no], obs_flag[batch_no]
         )

time: 845 us -> 809 us (0.957)
  blocking collectives: 83.8 us -> 51 us
    psum x4 -> x0, blocking collectives: 83.8 us -> none  [local(): lax.psum(jnp.sum(jnp.where(inside[None], picked, 0.0), axis=2) / pick_cou...]
    all_gather x0 -> x4, blocking collectives: none -> 51 us  [local(): shards = lax.all_gather(x, 'mem', axis=0, tiled=False)]
where the time goes in v1:
time: 809 us; the launch traced here: 808 us
  waiting for transfers between devices  598 us (74%)
  local copies, waits for them, and re-layouts  67.1 us (8%)
  blocking collectives  51 us (6%)
  other arithmetic  33.5 us (4%)
  starting transfers between devices  26.6 us (3%)
  matrix products  17.7 us (2%)
  between operations  14 us (2%)
    psum x4, waiting for transfers between devices, local(): inc_all, scl_all = lax.psum((placed_inc, placed_scl), 'cols')  570 us
    all_gather x4, blocking collectives, local(): shards = lax.all_gather(x, 'mem', axis=0, tiled=False)  51 us
    all_to_all x1, waiting for transfers between devices, local(): lax.all_to_all(state, 'mem', split_axis=1, concat_axis=0, tiled=True)  18.6 us
  transfers between devices with their start and end apart: 7, of which 6 were waited for; matrix products, arithmetic and copies ran while one was open for 4% of the time, Pallas kernels for 0%

profile of v1, /device:TPU:2, one launch (start us, length us, event | category | flops | bytes accessed | tf_op | source)
XLA Modules:
  0.0 808.0 jit_solution(6642324293531700160)
XLA Ops:
  10.0 7.9 scatter_fusion.1
  19.1 11.5 %all-to-all-start.2 = ((f32[4,32,2,2]{0,3,2,1:T(2,128)}), f32[4,32,2,2]{0,3,2,1:T(2,128)S(1)}, u32[]{:S(2)}, u32[]{:S(2)}) async-start(f32[4,32,2,2]{0,3,2,1:T(2,128)} %copy.270), calls=%async_computation.2 | async-start | bytes 131072 | tf_op jit(solution)/shard_map/all_to_all | solution.py:66
  31.4 7.9 scatter_fusion
  40.0 1.2 copy.348
  41.3 2.2 copy.253
  43.5 9.8 %all-to-all-start.1 = ((s32[4,32,2,7]{3,2,0,1:T(2,128)}), s32[4,32,2,7]{3,2,0,1:T(2,128)S(1)}, u32[]{:S(2)}, u32[]{:S(2)}) async-start(s32[4,32,2,7]{3,2,0,1:T(2,128)} %copy.261), calls=%async_computation.1 | async-start | bytes 262144 | tf_op jit(solution)/shard_map/all_to_all | solution.py:63
  54.2 9.5 %all-to-all-done.1 = s32[4,32,2,7]{3,2,0,1:T(2,128)S(1)} async-done(((s32[4,32,2,7]{3,2,0,1:T(2,128)}), s32[4,32,2,7]{3,2,0,1:T(2,128)S(1)}, u32[]{:S(2)}, u32[]{:S(2)}) %all-to-all-start.1) | async-done | bytes 7200 | tf_op jit(solution)/shard_map/all_to_all | solution.py:63
  63.7 4.8 all-to-all-start
  75.7 18.6 %all-to-all-done = f32[10,8,4096]{2,0,1:T(8,128)S(1)} async-done(((f32[10,8,4096]{2,0,1:T(8,128)}), f32[10,8,4096]{2,0,1:T(8,128)S(1)}, u32[]{:S(2)}, u32[]{:S(2)}) %all-to-all-start) | async-done | bytes 1310752 | tf_op jit(solution)/shard_map/all_to_all | solution.py:76
  94.5 1.8 copy.266
  96.3 2.4 gather_fusion
  99.8 12.2 %all-gather.4 = f32[8,80,64]{1,2,0:T(8,128)S(1)} all-gather(f32[1,80,64]{1,2,0:T(8,128)S(1)} %multiply_bitcast_fusion.3), channel_id=2, replica_groups=mesh['cols'=32,'mem'=8] {'mem'}, dimensions={0}, use_global_device_ids=true | all-gather | bytes 184320 | tf_op jit(solution)/shard_map/all_gather | solution.py:85
  113.0 1.2 scatter_custom_fusion.3
  122.2 1.3 broadcast_subtract_fusion
  123.5 138.5 %all-reduce.15.cloned.1.call-done = (f32[80,8,128]{2,0,1:T(8,128)}, f32[80,8,128]{2,0,1:T(8,128)}) async-done(((f32[80,8,128]{2,0,1:T(8,128)}, f32[80,8,128]{2,0,1:T(8,128)}), (f32[80,8,128]{2,0,1:T(8,128)}, f32[80,8,128]{2,0,1:T(8,128)})) %all-reduce.15.cloned.1.call-update) | async-done | bytes 655376 | tf_op jit(solution)/shard_map/psum | solution.py:93
  262.1 1.8 fusion.129
  264.4 2.1 fusion
  266.7 1.2 copy-done.4
  267.8 1.2 add.365
  269.0 2.8 copy.284
  271.9 2.4 gather_fusion.1
  275.3 12.8 %all-gather.5 = f32[8,80,64]{1,2,0:T(8,128)S(1)} all-gather(f32[1,80,64]{1,2,0:T(8,128)S(1)} %multiply_bitcast_fusion.2), channel_id=3, replica_groups=mesh['cols'=32,'mem'=8] {'mem'}, dimensions={0}, use_global_device_ids=true | all-gather | bytes 184320 | tf_op jit(solution)/shard_map/all_gather | solution.py:85
  289.1 1.8 scatter_custom_fusion.5
  291.0 2.0 copy.288
  292.9 1.8 scatter_custom_fusion.4
  294.7 2.0 copy.286
  298.9 1.8 copy.278
  300.7 2.7 reshape.689
  303.4 1.9 add_reduce_fusion
  305.4 138.1 %all-reduce.13.cloned.1.call-done = (f32[80,8,128]{2,0,1:T(8,128)}, f32[80,8,128]{2,0,1:T(8,128)}) async-done(((f32[80,8,128]{2,0,1:T(8,128)}, f32[80,8,128]{2,0,1:T(8,128)}), (f32[80,8,128]{2,0,1:T(8,128)}, f32[80,8,128]{2,0,1:T(8,128)})) %all-reduce.13.cloned.1.call-update) | async-done | bytes 655376 | tf_op jit(solution)/shard_map/psum | solution.py:93
  443.4 1.7 fusion.130
  445.7 3.9 fusion.126
  449.7 1.2 copy-done.5
  454.6 12.8 %all-gather.6 = f32[8,80,64]{1,2,0:T(8,128)S(1)} all-gather(f32[1,80,64]{1,2,0:T(8,128)S(1)} %multiply_bitcast_fusion.1), channel_id=4, replica_groups=mesh['cols'=32,'mem'=8] {'mem'}, dimensions={0}, use_global_device_ids=true | all-gather | bytes 184320 | tf_op jit(solution)/shard_map/all_gather | solution.py:85
  468.4 1.2 scatter_custom_fusion.7
  472.8 146.5 %all-reduce.11.cloned.1.call-done = (f32[80,8,128]{2,0,1:T(8,128)}, f32[80,8,128]{2,0,1:T(8,128)}) async-done(((f32[80,8,128]{2,0,1:T(8,128)}, f32[80,8,128]{2,0,1:T(8,128)}), (f32[80,8,128]{2,0,1:T(8,128)}, f32[80,8,128]{2,0,1:T(8,128)})) %all-reduce.11.cloned.1.call-update) | async-done | bytes 655376 | tf_op jit(solution)/shard_map/psum | solution.py:93
  619.4 1.7 fusion.131
  621.6 1.4 fusion.10
  623.1 1.2 copy-done.7
  624.3 1.2 add.390
  625.5 2.8 copy.308
  628.3 2.3 gather_fusion.3
  631.0 13.1 %all-gather.7 = f32[8,80,64]{1,2,0:T(8,128)S(1)} all-gather(f32[1,80,64]{1,2,0:T(8,128)S(1)} %multiply_bitcast_fusion), channel_id=5, replica_groups=mesh['cols'=32,'mem'=8] {'mem'}, dimensions={0}, use_global_device_ids=true | all-gather | bytes 184320 | tf_op jit(solution)/shard_map/all_gather | solution.py:85
  648.6 146.7 %all-reduce.9.cloned.1.call-done = (f32[80,8,128]{2,0,1:T(8,128)}, f32[80,8,128]{2,0,1:T(8,128)}) async-done(((f32[80,8,128]{2,0,1:T(8,128)}, f32[80,8,128]{2,0,1:T(8,128)}), (f32[80,8,128]{2,0,1:T(8,128)}, f32[80,8,128]{2,0,1:T(8,128)})) %all-reduce.9.cloned.1.call-update) | async-done | bytes 655376 | tf_op jit(solution)/shard_map/psum | solution.py:93
  795.4 1.7 fusion.132
  797.6 1.4 convolution_bitcast_fusion
  799.1 1.2 copy-done.8
  800.3 1.2 add.402
  (200 shorter events, 43.3 us)
Async XLA Ops:
  6.5 24.8 %copy-start.10 = (s32[4,32,2,7]{3,2,1,0:T(2,128)S(1)}, s32[4,32,2,7]{3,2,1,0:T(2,128)}, u32[]{:S(2)}) copy-start(s32[4,32,2,7]{3,2,1,0:T(2,128)} %constant.122.clone.1) | copy-start | bytes 21508
  6.5 24.1 %copy-start.18 = (s32[8,4,8]{2,1,0:T(4,128)S(1)}, s32[8,4,8]{2,1,0:T(4,128)}, u32[]{:S(2)}) copy-start(s32[8,4,8]{2,1,0:T(4,128)} %param.21) | copy-start | bytes 3076
  6.5 24.7 %copy-start.40 = (s32[4,32]{1,0:T(4,128)S(1)}, s32[4,32]{1,0:T(4,128)}, u32[]{:S(2)}) copy-start(s32[4,32]{1,0:T(4,128)} %param.20) | copy-start | bytes 1540
  6.5 24.7 %copy-start.21 = (s32[4,32,4]{1,2,0:T(4,128)S(1)}, s32[4,32,4]{1,2,0:T(4,128)}, u32[]{:S(2)}) copy-start(s32[4,32,4]{1,2,0:T(4,128)} %param.19) | copy-start | bytes 6148
  6.5 24.7 %copy-start.41 = (s32[4,32]{1,0:T(4,128)S(1)}, s32[4,32]{1,0:T(4,128)}, u32[]{:S(2)}) copy-start(s32[4,32]{1,0:T(4,128)} %param.18) | copy-start | bytes 1540
  18.0 22.0 %copy-start.11 = (f32[10,32768]{1,0:T(8,128)S(1)}, f32[10,32768]{1,0:T(8,128)}, u32[]{:S(2)}) copy-start(f32[10,32768]{1,0:T(8,128)} %param.14) | copy-start | bytes 3932164
  19.1 24.4 %all-to-all-start.2 = ((f32[4,32,2,2]{0,3,2,1:T(2,128)}), f32[4,32,2,2]{0,3,2,1:T(2,128)S(1)}, u32[]{:S(2)}, u32[]{:S(2)}) async-start(f32[4,32,2,2]{0,3,2,1:T(2,128)} %copy.270), calls=%async_computation.2 | async-start | bytes 131072 | tf_op jit(solution)/shard_map/all_to_all | solution.py:66
  43.5 20.2 %all-to-all-start.1 = ((s32[4,32,2,7]{3,2,0,1:T(2,128)}), s32[4,32,2,7]{3,2,0,1:T(2,128)S(1)}, u32[]{:S(2)}, u32[]{:S(2)}) async-start(s32[4,32,2,7]{3,2,0,1:T(2,128)} %copy.261), calls=%async_computation.1 | async-start | bytes 262144 | tf_op jit(solution)/shard_map/all_to_all | solution.py:63
  63.7 30.5 %all-to-all-start = ((f32[10,8,4096]{2,0,1:T(8,128)}), f32[10,8,4096]{2,0,1:T(8,128)S(1)}, u32[]{:S(2)}, u32[]{:S(2)}) async-start(f32[10,8,4096]{2,0,1:T(8,128)} %copy.253), calls=%async_computation | async-start | bytes 4194304 | tf_op jit(solution)/shard_map/all_to_all | solution.py:76
  68.6 193.5 %all-reduce.15.cloned.1.call-start = ((), (), s32[]{:S(2)}) async-start(), calls=%async_computation.6 | async-start | bytes 1310720 | tf_op jit(solution)/shard_map/psum | solution.py:93
  70.2 24.1 %copy-start.12 = (s32[1,64,4]{2,1,0:T(8,128)}, s32[1,64,4]{2,1,0:T(8,128)S(1)}, u32[]{:S(2)}) copy-start(s32[1,64,4]{2,1,0:T(8,128)S(1)} %get-tuple-element.79) | copy-start | bytes 3076
  70.2 24.1 %copy-start.14 = (s32[1,64,4]{2,1,0:T(8,128)}, s32[1,64,4]{2,1,0:T(8,128)S(1)}, u32[]{:S(2)}) copy-start(s32[1,64,4]{2,1,0:T(8,128)S(1)} %get-tuple-element.76) | copy-start | bytes 3076
  94.5 1.9 copy-start.3
  114.2 3.3 copy-start.19
  114.2 3.3 copy-start.20
  114.2 3.3 copy-start.22
  114.2 3.3 copy-start.23
  114.2 3.3 copy-start.35
  114.2 3.3 copy-start.36
  114.2 3.9 copy-start.15
  114.2 4.5 copy-start.13
  115.2 5.8 copy-start.38
  115.2 5.9 copy-start.24
  117.3 326.2 %all-reduce.13.cloned.1.call-start = ((), (), s32[]{:S(2)}) async-start(), calls=%async_computation.5 | async-start | bytes 1310720 | tf_op jit(solution)/shard_map/psum | solution.py:93
  122.0 1.5 copy-start.1
  262.0 2.3 copy-start.9
  266.5 1.3 copy-start.4
  271.9 17.3 %copy-start.31 = (f32[64]{0:T(128)S(1)}, f32[64]{0:T(128)}, u32[]{:S(2)}) copy-start(f32[64]{0:T(128)} %get-tuple-element.40) | copy-start | bytes 772
  290.9 6.0 copy-start.25
  290.9 6.0 copy-start.27
  291.0 6.0 copy-start.28
  291.0 6.0 copy-start.29
  291.0 6.6 copy-start.39
  296.7 322.7 %all-reduce.11.cloned.1.call-start = ((), (), s32[]{:S(2)}) async-start(), calls=%async_computation.4 | async-start | bytes 1310720 | tf_op jit(solution)/shard_map/psum | solution.py:93
  305.3 140.3 %copy-start.2 = (f32[80,8,512]{2,1,0:T(8,128)S(1)}, f32[80,8,512]{2,1,0:T(8,128)}, u32[]{:S(2)}) copy-start(f32[80,8,512]{2,1,0:T(8,128)} %copy-done.1) | copy-start | bytes 3932164
  449.6 1.3 copy-start.5
  469.6 3.1 copy-start.37
  469.6 3.2 copy-start.26
  471.7 149.4 %copy-start.17 = (s32[8,1,8]{2,1,0:T(1,128)S(1)}, s32[8,1,8]{2,1,0:T(1,128)}, u32[]{:S(2)}) copy-start(s32[8,1,8]{2,1,0:T(1,128)} %get-tuple-element.83) | copy-start | bytes 772
  472.6 149.0 %copy-start = (f32[80,8,512]{2,0,1:T(8,128)S(1)}, f32[80,8,512]{2,0,1:T(8,128)}, u32[]{:S(2)}) copy-start(f32[80,8,512]{2,0,1:T(8,128)} %get-tuple-element.71) | copy-start | bytes 3932164
  472.6 322.7 %all-reduce.9.cloned.1.call-start = ((), (), s32[]{:S(2)}) async-start(), calls=%async_computation.3 | async-start | bytes 1310720 | tf_op jit(solution)/shard_map/psum | solution.py:93
  623.0 1.3 copy-start.7
  625.5 5.1 copy-start.34
  628.3 16.0 %copy-start.32 = (f32[64]{0:T(128)S(1)}, f32[64]{0:T(128)}, u32[]{:S(2)}) copy-start(f32[64]{0:T(128)} %get-tuple-element.50) | copy-start | bytes 772
  628.3 16.1 %copy-start.33 = (f32[64]{0:T(128)S(1)}, f32[64]{0:T(128)}, u32[]{:S(2)}) copy-start(f32[64]{0:T(128)} %get-tuple-element.51) | copy-start | bytes 772
  628.3 16.1 %copy-start.30 = (f32[64]{0:T(128)S(1)}, f32[64]{0:T(128)}, u32[]{:S(2)}) copy-start(f32[64]{0:T(128)} %get-tuple-element.38) | copy-start | bytes 772
  647.6 149.4 %copy-start.16 = (s32[8,1,8]{2,1,0:T(1,128)S(1)}, s32[8,1,8]{2,1,0:T(1,128)}, u32[]{:S(2)}) copy-start(s32[8,1,8]{2,1,0:T(1,128)} %get-tuple-element.82) | copy-start | bytes 772
  799.0 1.3 copy-start.8
  (1 other events, 1.1 us)
Sparse Core Ops, SparseCore 0:
  117.4 144.6 all-reduce.14
  296.8 146.5 all-reduce.12
  472.7 146.5 all-reduce.10
  648.7 146.5 all-reduce.8
